TPU v7x, 256 devices: a whole 4x4x8 slice. The times are simulated.
256 devices in a mesh: cable: 4 (over y), fx: 32 (over z, x), fz: 2 (over core).
Axes of the slice: x: 4, y: 4, z: 8, core: 2. Of those that a mesh axis runs over, the one named last changes fastest.
Arguments:
- velocity: float32 [3, 256, 64, 256], P(None, 'fx', 'cable', 'fz'), may hold values from -6 to 6
- viscosity: float32 [256, 64, 256], P('fx', 'cable', 'fz'), may hold values from 0.02 to 0.15
- disp_init: float32 [3, 16384], P(None, ('cable', 'fx', 'fz')), may hold values from -3 to 3
- rest_shape: float32 [3, 16384], P(None, ('cable', 'fx', 'fz')), may hold values from -6 to 6
- compliance: float32 [16384], P(('cable', 'fx', 'fz')), may hold values from 0.5 to 2
- stencil_weights: float32 [3, 12, 16384], P(None, None, ('cable', 'fx', 'fz')), may hold values from 0.05 to 0.45
- anchor: int32 [3, 16384], P(None, ('cable', 'fx', 'fz')), may hold values from 0 to 9852, as said below
- owners: int32 [3, 16384], P(None, ('cable', 'fx', 'fz')), may hold values from 0 to 63, as said below
Outputs:
- disp_next: float32 [3, 16384], P(None, ('cable', 'fx', 'fz'))
- velocity_out: float32 [3, 256, 64, 256], P(None, 'fx', 'cable', 'fz')
Inputs may be any that keep to these rules, and one draw needn't show every extreme that they name: `owners`: the owner's number is fx * 2 + fz of a fluid block in the segment's own cable group. Among the 64 segments of one device (aligned blocks of 64 segments), at most 4 name the same owner in one iteration; in every iteration one owner is named by exactly 4 segments of every device of each group. `anchor`: the cell is numbered (x * 16 + y) * 128 + z in the owner's block, with x <= 4, y <= 12 and z <= 124, so the 4 x 4 x 4 stencil lies inside that block.
All inputs are finite; a program needn't handle non-finite values.
Results may differ from a plain program's by a relative error of at most 0.0003.
Values sent between devices are 32-bit elements; how exact they have to be, the bound alone decides.
No kernel may reach another device: no remote copies, remote signals or barrier semaphores. Data moves between devices by JAX's collectives and lax.ppermute only.
A program may use at most 64 MiB of HBM per device.

v0:
```python
import jax
import jax.numpy as jnp
from jax import lax
from jax.sharding import PartitionSpec as P

ITERS = 3
spread_gain = 16.0
drag_coeff = 0.05
relaxation = 0.5
ridge_share = 0.01


def with_halo(cells, sides, width):
    for axis, dim in sides:
        count = lax.axis_size(axis)
        ends = count - 1
        head = lax.slice_in_dim(cells, 0, width, axis=dim)
        tail = lax.slice_in_dim(cells, cells.shape[dim] - width, cells.shape[dim], axis=dim)
        cells = jnp.concatenate(
            [
                lax.ppermute(tail, axis, [(i, (i + 1) % count) for i in range(ends)]),
                cells,
                lax.ppermute(head, axis, [((i + 1) % count, i) for i in range(ends)]),
            ],
            axis=dim,
        )
    return cells


def stencil_table(weights):
    table = (
        weights[0:4][:, None, None, :]
        * weights[4:8][None, :, None, :]
        * weights[8:12][None, None, :, :]
    )
    return table.reshape(64, weights.shape[1])


def face_sum(padded):
    beside = padded[:, 2:, 1:-1, 1:-1] + padded[:, :-2, 1:-1, 1:-1]
    beside = beside + padded[:, 1:-1, 2:, 1:-1] + padded[:, 1:-1, :-2, 1:-1]
    beside = beside + padded[:, 1:-1, 1:-1, 2:] + padded[:, 1:-1, 1:-1, :-2]
    return beside


def solve_small(gram, width):
    square = gram[:width, :width]
    target = gram[:width, width]
    shift = ridge_share * jnp.trace(square) / width + 1e-06
    if width == 1:
        return [-target[0] / (square[0, 0] + shift)]
    first = square[0, 0] + shift
    second = square[1, 1] + shift
    cross = square[0, 1]
    determinant = first * second - cross * cross
    return [
        -(second * target[0] - cross * target[1]) / determinant,
        -(first * target[1] - cross * target[0]) / determinant,
    ]


def body(velocity, viscosity, disp_init, rest_shape, compliance, stencil_weights, anchor, owners):
    member = lax.axis_index(("fx", "fz"))
    seg_count = disp_init.shape[1]
    seg_total = seg_count * lax.axis_size(("cable", "fx", "fz"))
    position = lax.axis_index(("cable", "fx", "fz")) * seg_count + jnp.arange(
        seg_count, dtype=jnp.int32
    )
    tension_ramp = 1.0 + 2.0 * position.astype(jnp.float32) / seg_total
    size_x, size_y, size_z = viscosity.shape
    cells = size_x * size_y * size_z
    slot_total = 4 * seg_count
    steps_one = jnp.arange(4, dtype=jnp.int32)
    offsets = (
        (steps_one[:, None, None] * size_y + steps_one[None, :, None]) * size_z
        + steps_one[None, None, :]
    ).reshape(64)
    current = disp_init
    residuals = []
    responses = []
    velocity_out = velocity
    for iteration in range(ITERS):
        corner_row = anchor[iteration].astype(jnp.float32)[None]
        payload = jnp.concatenate([current, stencil_weights[iteration], corner_row], axis=0)
        owner_row = owners[iteration].astype(jnp.float32)[None]
        everyone = lax.all_gather(
            jnp.concatenate([payload, owner_row], axis=0), ("fx", "fz"), axis=1, tiled=True
        )
        owned = (everyone[16].astype(jnp.int32) == member).astype(jnp.int32)
        rank = jnp.cumsum(owned) - owned
        slot_place = jnp.where(owned > 0, rank, slot_total)
        compact = (
            jnp.zeros((16, slot_total + 1), jnp.float32)
            .at[:, slot_place]
            .set(everyone[0:16])[:, :slot_total]
        )
        corner = compact[15].astype(jnp.int32)
        cell_index = corner[None, :] + offsets[:, None]
        stencil = stencil_table(compact[3:15])
        spread_terms = spread_gain * stencil[None] * compact[0:3][:, None, :]
        forcing = (
            jnp.zeros((3, cells), jnp.float32)
            .at[:, cell_index.reshape(-1)]
            .add(spread_terms.reshape(3, -1))
        )
        forcing_field = forcing.reshape(velocity.shape)
        u_star = velocity + forcing_field
        padded = with_halo(u_star, (("cable", 2), ("fx", 1), ("fz", 3)), 1)
        beside = face_sum(padded)
        laplace = beside - 6.0 * u_star
        speed = jnp.sqrt(1.0 + jnp.sum(u_star * u_star, axis=0, keepdims=True))
        u_new = u_star + viscosity[None] * laplace - drag_coeff * u_star * speed
        picked = u_new.reshape(3, cells)[:, cell_index]
        sampled = jnp.sum(stencil[None] * picked, axis=1)
        widened = jnp.concatenate([sampled, jnp.zeros((3, 1), jnp.float32)], axis=1)
        spread_back = widened[:, slot_place]
        returned = lax.psum_scatter(spread_back, ("fx", "fz"), scatter_dimension=1, tiled=True)
        response = rest_shape + compliance[None] * tension_ramp[None] * returned
        response, velocity_out = (response, u_new)
        residual = response - current
        if iteration == 0:
            following = current + relaxation * residual
        else:
            columns = [residual - earlier for earlier in residuals]
            changes = [response - earlier for earlier in responses]
            matrix = jnp.stack(columns + [residual]).reshape(iteration + 1, -1)
            partial_gram = jnp.dot(matrix, matrix.T, precision=lax.Precision.HIGHEST)
            gram = lax.psum(partial_gram, ("cable", "fx", "fz"))
            coefs = solve_small(gram, iteration)
            following = response
            for column in range(iteration):
                following = following + coefs[column] * changes[column]
        residuals.append(residual)
        responses.append(response)
        current = following
    return (current, velocity_out)


def solution(mesh):
    placed = (
        P(None, "fx", "cable", "fz"),
        P("fx", "cable", "fz"),
        P(None, ("cable", "fx", "fz")),
        P(None, ("cable", "fx", "fz")),
        P(("cable", "fx", "fz")),
        P(None, None, ("cable", "fx", "fz")),
        P(None, ("cable", "fx", "fz")),
        P(None, ("cable", "fx", "fz")),
    )
    return jax.shard_map(
        body,
        mesh=mesh,
        in_specs=placed,
        out_specs=(P(None, ("cable", "fx", "fz")), P(None, "fx", "cable", "fz")),
        check_vma=False,
    )
```

profile of v0, /device:TPU:1, one launch (start us, length us, event | category | flops | bytes accessed | tf_op | source)
XLA Modules:
  0.0 1473.1 jit_solution(890402977995218385)
XLA Ops:
  9.5 55.1 %all-gather = f32[64,64,17]{1,2,0:T(8,128)S(1)} all-gather(f32[1,64,17]{1,2,0:T(8,128)S(1)} %maximum_bitcast_fusion), channel_id=1, replica_groups=mesh['cable'=4,'fx'=32,'fz'=2] {'fx','fz'}, dimensions={0}, use_global_device_ids=true | all-gather | bytes 282880 | tf_op jit(solution)/shard_map/all_gather | solution.py:86
  66.2 10.6 scatter_custom_fusion
  78.0 4.6 bitcast_multiply_fusion.2
  82.6 109.0 %scatter_custom_fusion.1 = f32[3,16384]{0,1:T(8,128)} fusion(s32[16384]{0:T(1024)S(1)} %bitcast.195, f32[3,16384]{0,1:T(8,128)} %bitcast_multiply_fusion.2, f32[]{:T(128)} %constant.30.clone.1), kind=kCustom, calls=%fused_computation.18 | custom fusion | flops 49152 | bytes 393220 | tf_op jit(solution)/shard_map/scatter-add | solution.py:104
  191.6 5.3 copy.63
  196.9 2.8 collective-permute-start
  201.2 3.2 collective-permute-done.1
  204.4 2.3 collective-permute-start.3
  208.1 3.4 collective-permute-done.2
  211.7 4.9 collective-permute-start.4
  220.6 4.6 copy.64
  225.2 57.8 %gather_fusion = f32[16384,3]{1,0:T(8,128)} fusion(f32[3,16384]{0,1:T(8,128)} %bitcast.156, s32[16384]{0:T(1024)S(1)} %broadcast_clamp_fusion.2), kind=kCustom, calls=%fused_computation | custom fusion | bytes 458752 | tf_op jit(solution)/shard_map/gather | solution.py:113
  283.0 5.3 multiply_reduce_fusion.2
  288.3 14.1 gather_fusion.1
  302.5 137.5 %reduce-scatter.10.cloned.1.call-done = f32[64,3]{1,0:T(8,128)} async-done(((f32[4096,3]{1,0:T(8,128)}), f32[64,3]{1,0:T(8,128)}) %reduce-scatter.10.cloned.1.call-update) | async-done | bytes 784
  440.9 55.0 %all-gather.1 = f32[64,64,17]{1,2,0:T(8,128)S(1)} all-gather(f32[1,64,17]{1,2,0:T(8,128)S(1)} %maximum_bitcast_fusion.1), channel_id=1, replica_groups=mesh['cable'=4,'fx'=32,'fz'=2] {'fx','fz'}, dimensions={0}, use_global_device_ids=true | all-gather | bytes 282880 | tf_op jit(solution)/shard_map/all_gather | solution.py:86
  497.5 10.6 scatter_custom_fusion.2
  509.2 4.6 bitcast_multiply_fusion.1
  513.8 108.7 %scatter_custom_fusion.3 = f32[3,16384]{0,1:T(8,128)} fusion(s32[16384]{0:T(1024)S(1)} %bitcast.196, f32[3,16384]{0,1:T(8,128)} %bitcast_multiply_fusion.1, f32[]{:T(128)} %constant.30.clone.1), kind=kCustom, calls=%fused_computation.15 | custom fusion | flops 49152 | bytes 393220 | tf_op jit(solution)/shard_map/scatter-add | solution.py:104
  622.5 5.2 copy.71
  627.8 3.3 collective-permute-start.6
  632.4 3.1 collective-permute-done.7
  635.5 2.0 collective-permute-start.9
  638.9 3.4 collective-permute-done.8
  642.5 5.1 collective-permute-start.10
  649.1 2.1 collective-permute-done.11
  651.5 4.6 copy.72
  656.1 57.8 %gather_fusion.2 = f32[16384,3]{1,0:T(8,128)} fusion(f32[3,16384]{0,1:T(8,128)} %bitcast.157, s32[16384]{0:T(1024)S(1)} %broadcast_clamp_fusion.1), kind=kCustom, calls=%fused_computation.2 | custom fusion | bytes 458752 | tf_op jit(solution)/shard_map/gather | solution.py:113
  713.9 5.3 multiply_reduce_fusion.1
  719.2 14.1 gather_fusion.3
  733.3 137.5 %reduce-scatter.12.cloned.1.call-done = f32[64,3]{1,0:T(8,128)} async-done(((f32[4096,3]{1,0:T(8,128)}), f32[64,3]{1,0:T(8,128)}) %reduce-scatter.12.cloned.1.call-update) | async-done | bytes 784
  871.8 79.6 %psum.14 = f32[2,2]{1,0:T(2,128)S(1)} all-reduce(f32[2,2]{1,0:T(2,128)S(1)} %convolution_bitcast_fusion.1), channel_id=1, replica_groups=mesh['cable'=4,'fx'=32,'fz'=2] {'cable','fx','fz'}, use_global_device_ids=true, to_apply=%region_14.15 | all-reduce | flops 4 | bytes 32 | tf_op jit(solution)/shard_map/psum | solution.py:128
  954.0 50.5 %all-gather.2 = f32[64,64,17]{1,2,0:T(8,128)S(1)} all-gather(f32[1,64,17]{1,2,0:T(8,128)S(1)} %maximum_bitcast_fusion.2), channel_id=1, replica_groups=mesh['cable'=4,'fx'=32,'fz'=2] {'fx','fz'}, dimensions={0}, use_global_device_ids=true | all-gather | bytes 282880 | tf_op jit(solution)/shard_map/all_gather | solution.py:86
  1006.2 10.6 scatter_custom_fusion.4
  1017.9 4.6 bitcast_multiply_fusion
  1022.4 109.0 %scatter_custom_fusion.5 = f32[3,16384]{0,1:T(8,128)} fusion(s32[16384]{0:T(1024)S(1)} %bitcast.197, f32[3,16384]{0,1:T(8,128)} %bitcast_multiply_fusion, f32[]{:T(128)} %constant.30.clone.1), kind=kCustom, calls=%fused_computation.12 | custom fusion | flops 49152 | bytes 393220 | tf_op jit(solution)/shard_map/scatter-add | solution.py:104
  1131.4 5.2 copy.80
  1139.3 3.1 collective-permute-done.13
  1142.5 2.6 collective-permute-start.15
  1146.4 3.4 collective-permute-done.14
  1150.0 4.9 collective-permute-start.16
  1156.3 2.2 collective-permute-done.17
  1158.8 4.6 copy.81
  1163.5 57.8 %gather_fusion.4 = f32[16384,3]{1,0:T(8,128)} fusion(f32[3,16384]{0,1:T(8,128)} %bitcast.158, s32[16384]{0:T(1024)S(1)} %broadcast_clamp_fusion), kind=kCustom, calls=%fused_computation.4 | custom fusion | bytes 458752 | tf_op jit(solution)/shard_map/gather | solution.py:113
  1221.2 5.2 multiply_reduce_fusion
  1226.5 14.1 gather_fusion.5
  1240.6 136.3 %reduce-scatter.14.cloned.1.call-done = f32[64,3]{1,0:T(8,128)} async-done(((f32[4096,3]{1,0:T(8,128)}), f32[64,3]{1,0:T(8,128)}) %reduce-scatter.14.cloned.1.call-update) | async-done | bytes 784
  1378.0 79.5 %psum.15 = f32[3,3]{1,0:T(4,128)S(1)} all-reduce(f32[3,3]{1,0:T(4,128)S(1)} %convolution_bitcast_fusion), channel_id=1, replica_groups=mesh['cable'=4,'fx'=32,'fz'=2] {'cable','fx','fz'}, use_global_device_ids=true, to_apply=%region_22.23 | all-reduce | flops 9 | bytes 72 | tf_op jit(solution)/shard_map/psum | solution.py:128
  (173 shorter events, 33.2 us)
Async XLA Ops:
  7.2 432.8 %reduce-scatter.10.cloned.1.call-start = ((), (), s32[]{:S(2)}) async-start(), calls=%async_computation.3 | async-start | bytes 2129920
  191.6 5.3 copy-start
  191.6 28.7 %copy-start.2 = (f32[8,16,128]{2,1,0:T(8,128)S(1)}, f32[8,16,128]{2,1,0:T(8,128)}, u32[]{:S(2)}) copy-start(f32[8,16,128]{2,1,0:T(8,128)} %param.9) | copy-start | bytes 196612
  196.9 4.3 collective-permute-start
  199.7 4.7 collective-permute-start.1
  204.4 3.7 collective-permute-start.3
  206.8 4.7 collective-permute-start.2
  211.7 6.8 collective-permute-start.4
  216.7 3.6 collective-permute-start.5
  225.2 77.3 %copy-start.5 = (f32[64]{0:T(128)S(1)}, f32[64]{0:T(128)}, u32[]{:S(2)}) copy-start(f32[64]{0:T(128)} %param.12) | copy-start | bytes 772
  225.2 215.6 %copy-start.3 = (f32[3,64]{1,0:T(4,128)S(1)}, f32[3,64]{1,0:T(4,128)}, u32[]{:S(2)}) copy-start(f32[3,64]{1,0:T(4,128)} %param.11) | copy-start | bytes 2308
  225.2 215.6 %copy-start.4 = (f32[3,64]{1,0:T(4,128)S(1)}, f32[3,64]{1,0:T(4,128)}, u32[]{:S(2)}) copy-start(f32[3,64]{1,0:T(4,128)} %param.10) | copy-start | bytes 2308
  302.4 568.4 %reduce-scatter.12.cloned.1.call-start = ((), (), s32[]{:S(2)}) async-start(), calls=%async_computation.4 | async-start | bytes 2129920
  627.8 4.6 collective-permute-start.6
  631.1 4.4 collective-permute-start.7
  635.5 3.3 collective-permute-start.9
  637.5 4.7 collective-permute-start.8
  642.5 6.6 collective-permute-start.10
  647.6 3.6 collective-permute-start.11
  733.3 643.7 %reduce-scatter.14.cloned.1.call-start = ((), (), s32[]{:S(2)}) async-start(), calls=%async_computation.5 | async-start | bytes 2129920
  1136.7 2.6 collective-permute-start.12
  1138.0 4.4 collective-permute-start.13
  1142.5 3.9 collective-permute-start.15
  1145.0 4.7 collective-permute-start.14
  1150.0 6.3 collective-permute-start.16
  1154.9 3.6 collective-permute-start.17
  1158.8 67.7 %copy-start.1 = (f32[3,8,16,128]{3,2,1,0:T(8,128)}, f32[3,8,16,128]{3,2,1,0:T(8,128)S(1)}, u32[]{:S(2)}) copy-start(f32[3,8,16,128]{3,2,1,0:T(8,128)S(1)} %fusion.13) | copy-start | bytes 589828
Sparse Core Ops, SparseCore 0:
  302.5 137.4 reduce-scatter.9
  733.4 137.3 reduce-scatter.11
  1240.8 136.1 reduce-scatter.13
where the time goes:
time: 1480 us; the launch traced here: 1470 us
  waiting for transfers between devices  437 us (30%)
  other arithmetic  363 us (25%)
  blocking collectives  320 us (22%)
  local copies, waits for them, and re-layouts  287 us (19%)
  starting transfers between devices  41.6 us (3%)
  between operations  23.9 us (2%)
    unnamed x6, waiting for transfers between devices  411 us
    scatter-add x3, other arithmetic, body(): forcing = jnp.zeros((3, cells), jnp.float32).at[:, cell_index.reshape(-1)...  327 us
    gather x3, local copies, waits for them, and re-layouts, body(): picked = u_new.reshape(3, cells)[:, cell_index]  173 us
    all_gather x3, blocking collectives, body(): lax.all_gather(jnp.concatenate([payload, owner_row], axis=0), ('fx', 'fz'...  161 us
    psum x2, blocking collectives, body(): gram = lax.psum(partial_gram, ('cable', 'fx', 'fz'))  159 us
    gather x3, local copies, waits for them, and re-layouts, body(): spread_back = widened[:, slot_place]  42.3 us
    scatter x3, local copies, waits for them, and re-layouts, body(): compact = jnp.zeros((16, slot_total + 1), jnp.float32).at[:, slot_place]....  31.9 us
  transfers between devices with their start and end apart: 21, of which 12 were waited for; matrix products, arithmetic and copies ran while one was open for 0% of the time, Pallas kernels for 0%

commit v1 on v0

--- a/solution.py
+++ b/solution.py
@@ -83,9 +83,9 @@
         corner_row = anchor[iteration].astype(jnp.float32)[None]
         payload = jnp.concatenate([current, stencil_weights[iteration], corner_row], axis=0)
         owner_row = owners[iteration].astype(jnp.float32)[None]
-        everyone = lax.all_gather(
-            jnp.concatenate([payload, owner_row], axis=0), ("fx", "fz"), axis=1, tiled=True
-        )
+        x = jnp.concatenate([payload, owner_row], axis=0)
+        repeated = jnp.stack([x] * lax.axis_size(("fx", "fz")))
+        everyone = jnp.concatenate(lax.all_to_all(repeated, ("fx", "fz"), 0, 0), axis=1)
         owned = (everyone[16].astype(jnp.int32) == member).astype(jnp.int32)
         rank = jnp.cumsum(owned) - owned
         slot_place = jnp.where(owned > 0, rank, slot_total)

time: 1480 us -> 1400 us (0.946)
  blocking collectives: 320 us -> 207 us
  starting transfers between devices: 41.6 us -> 56.6 us
    all_gather x3 -> x0, blocking collectives: 161 us -> none  [body(): lax.all_gather(jnp.concatenate([payload, owner_row], axis=0), ('fx', 'fz'...]
    all_to_all x0 -> x2, blocking collectives: none -> 47.4 us  [body(): lax.all_to_all(repeated, ('fx', 'fz'), 0, 0)]
  transfers between devices with their start and end apart: 21 -> 22, of which waited for: 12 -> 13; matrix products, arithmetic and copies ran while one was open for 0% -> 0% of each run, Pallas kernels for 0% -> 0%
where the time goes in v1:
time: 1400 us; the launch traced here: 1390 us
  waiting for transfers between devices  445 us (32%)
  other arithmetic  369 us (26%)
  local copies, waits for them, and re-layouts  292 us (21%)
  blocking collectives  207 us (15%)
  starting transfers between devices  56.6 us (4%)
  between operations  23.9 us (2%)
    unnamed x6, waiting for transfers between devices  406 us
    scatter-add x3, other arithmetic, body(): forcing = jnp.zeros((3, cells), jnp.float32).at[:, cell_index.reshape(-1)...  327 us
    gather x3, local copies, waits for them, and re-layouts, body(): picked = u_new.reshape(3, cells)[:, cell_index]  173 us
    psum x2, blocking collectives, body(): gram = lax.psum(partial_gram, ('cable', 'fx', 'fz'))  159 us
    all_to_all x2, blocking collectives, body(): lax.all_to_all(repeated, ('fx', 'fz'), 0, 0)  47.4 us
    gather x3, local copies, waits for them, and re-layouts, body(): spread_back = widened[:, slot_place]  42.3 us
    scatter x3, local copies, waits for them, and re-layouts, body(): compact = jnp.zeros((16, slot_total + 1), jnp.float32).at[:, slot_place]....  31.9 us
  transfers between devices with their start and end apart: 22, of which 13 were waited for; matrix products, arithmetic and copies ran while one was open for 0% of the time, Pallas kernels for 0%

profile of v1, /device:TPU:1, one launch (start us, length us, event | category | flops | bytes accessed | tf_op | source)
XLA Modules:
  0.0 1393.5 jit_solution(18408914018322801410)
XLA Ops:
  10.5 13.0 all-to-all-start
  23.8 13.4 all-to-all-done
  42.3 10.6 scatter_custom_fusion
  54.0 4.6 bitcast_multiply_fusion.2
  58.6 109.0 %scatter_custom_fusion.1 = f32[3,16384]{0,1:T(8,128)} fusion(s32[16384]{0:T(1024)S(1)} %bitcast.165, f32[3,16384]{0,1:T(8,128)} %bitcast_multiply_fusion.2, f32[]{:T(128)} %constant.30.clone.1), kind=kCustom, calls=%fused_computation.18 | custom fusion | flops 49152 | bytes 393220 | tf_op jit(solution)/shard_map/scatter-add | solution.py:104
  167.6 5.3 copy.84
  172.9 2.8 collective-permute-start
  177.0 3.4 collective-permute-done.1
  183.8 3.4 collective-permute-done.2
  187.4 5.2 collective-permute-start.4
  193.9 2.2 collective-permute-done.5
  196.5 4.6 copy.85
  201.1 57.8 %gather_fusion = f32[16384,3]{1,0:T(8,128)} fusion(f32[3,16384]{0,1:T(8,128)} %bitcast.123, s32[16384]{0:T(1024)S(1)} %broadcast_clamp_fusion.2), kind=kCustom, calls=%fused_computation | custom fusion | bytes 458752 | tf_op jit(solution)/shard_map/gather | solution.py:113
  258.9 5.3 multiply_reduce_fusion.2
  264.2 14.1 %gather_fusion.1 = f32[4096,3]{1,0:T(8,128)} fusion(f32[3,257]{0,1:T(8,128)S(1)} %concatenate.102, s32[4096]{0:T(1024)S(1)} %broadcast_clamp_fusion.5), kind=kCustom, calls=%fused_computation.1 | custom fusion | bytes 114688 | tf_op jit(solution)/shard_map/gather | solution.py:116
  278.9 135.6 %reduce-scatter.10.cloned.1.call-done = f32[64,3]{1,0:T(8,128)} async-done(((f32[4096,3]{1,0:T(8,128)}), f32[64,3]{1,0:T(8,128)}) %reduce-scatter.10.cloned.1.call-update) | async-done | bytes 784
  415.8 26.3 %all_to_all.15 = f32[64,1,1088]{2,1,0:T(1,128)S(1)} all-to-all(f32[64,1,1088]{2,1,0:T(1,128)S(1)} %reshape.924), channel_id=1, replica_groups=mesh['cable'=4,'fx'=32,'fz'=2] {'fx','fz'}, dimensions={0} | all-to-all | bytes 557056 | tf_op jit(solution)/shard_map/all_to_all | solution.py:88
  446.2 10.6 scatter_custom_fusion.2
  457.9 4.6 bitcast_multiply_fusion.1
  462.4 108.7 %scatter_custom_fusion.3 = f32[3,16384]{0,1:T(8,128)} fusion(s32[16384]{0:T(1024)S(1)} %bitcast.166, f32[3,16384]{0,1:T(8,128)} %bitcast_multiply_fusion.1, f32[]{:T(128)} %constant.30.clone.1), kind=kCustom, calls=%fused_computation.15 | custom fusion | flops 49152 | bytes 393220 | tf_op jit(solution)/shard_map/scatter-add | solution.py:104
  571.2 5.2 copy.92
  576.5 3.5 collective-permute-start.6
  581.3 3.1 collective-permute-done.7
  584.4 2.6 collective-permute-start.9
  588.3 3.4 collective-permute-done.8
  591.9 5.3 collective-permute-start.10
  601.1 4.6 copy.93
  605.7 57.8 %gather_fusion.2 = f32[16384,3]{1,0:T(8,128)} fusion(f32[3,16384]{0,1:T(8,128)} %bitcast.124, s32[16384]{0:T(1024)S(1)} %broadcast_clamp_fusion.1), kind=kCustom, calls=%fused_computation.2 | custom fusion | bytes 458752 | tf_op jit(solution)/shard_map/gather | solution.py:113
  663.5 5.3 multiply_reduce_fusion.1
  668.8 14.1 %gather_fusion.3 = f32[4096,3]{1,0:T(8,128)} fusion(f32[3,257]{0,1:T(8,128)S(1)} %concatenate.112, s32[4096]{0:T(1024)S(1)} %broadcast_clamp_fusion.4), kind=kCustom, calls=%fused_computation.3 | custom fusion | bytes 114688 | tf_op jit(solution)/shard_map/gather | solution.py:116
  683.0 135.3 %reduce-scatter.12.cloned.1.call-done = f32[64,3]{1,0:T(8,128)} async-done(((f32[4096,3]{1,0:T(8,128)}), f32[64,3]{1,0:T(8,128)}) %reduce-scatter.12.cloned.1.call-update) | async-done | bytes 784
  819.2 79.7 %psum.14 = f32[2,2]{1,0:T(2,128)S(1)} all-reduce(f32[2,2]{1,0:T(2,128)S(1)} %convolution_bitcast_fusion.1), channel_id=1, replica_groups=mesh['cable'=4,'fx'=32,'fz'=2] {'cable','fx','fz'}, use_global_device_ids=true, to_apply=%region_14.15 | all-reduce | flops 4 | bytes 32 | tf_op jit(solution)/shard_map/psum | solution.py:128
  901.9 21.1 %all_to_all.16 = f32[64,1,1088]{2,1,0:T(1,128)S(1)} all-to-all(f32[64,1,1088]{2,1,0:T(1,128)S(1)} %reshape.926), channel_id=1, replica_groups=mesh['cable'=4,'fx'=32,'fz'=2] {'fx','fz'}, dimensions={0} | all-to-all | bytes 557056 | tf_op jit(solution)/shard_map/all_to_all | solution.py:88
  927.1 10.6 scatter_custom_fusion.4
  938.9 4.6 bitcast_multiply_fusion
  943.4 109.0 %scatter_custom_fusion.5 = f32[3,16384]{0,1:T(8,128)} fusion(s32[16384]{0:T(1024)S(1)} %bitcast.167, f32[3,16384]{0,1:T(8,128)} %bitcast_multiply_fusion, f32[]{:T(128)} %constant.30.clone.1), kind=kCustom, calls=%fused_computation.12 | custom fusion | flops 49152 | bytes 393220 | tf_op jit(solution)/shard_map/scatter-add | solution.py:104
  1052.4 5.2 copy.101
  1057.7 2.4 collective-permute-start.12
  1061.4 3.1 collective-permute-done.13
  1064.6 2.3 collective-permute-start.15
  1068.2 3.4 collective-permute-done.14
  1071.8 5.2 collective-permute-start.16
  1080.9 4.6 copy.102
  1085.5 57.8 %gather_fusion.4 = f32[16384,3]{1,0:T(8,128)} fusion(f32[3,16384]{0,1:T(8,128)} %bitcast.125, s32[16384]{0:T(1024)S(1)} %broadcast_clamp_fusion), kind=kCustom, calls=%fused_computation.4 | custom fusion | bytes 458752 | tf_op jit(solution)/shard_map/gather | solution.py:113
  1143.3 5.2 multiply_reduce_fusion
  1148.6 14.1 %gather_fusion.5 = f32[4096,3]{1,0:T(8,128)} fusion(f32[3,257]{0,1:T(8,128)S(1)} %concatenate.122, s32[4096]{0:T(1024)S(1)} %broadcast_clamp_fusion.3), kind=kCustom, calls=%fused_computation.5 | custom fusion | bytes 114688 | tf_op jit(solution)/shard_map/gather | solution.py:116
  1162.7 134.6 %reduce-scatter.14.cloned.1.call-done = f32[64,3]{1,0:T(8,128)} async-done(((f32[4096,3]{1,0:T(8,128)}), f32[64,3]{1,0:T(8,128)}) %reduce-scatter.14.cloned.1.call-update) | async-done | bytes 784
  1298.3 79.6 %psum.15 = f32[3,3]{1,0:T(4,128)S(1)} all-reduce(f32[3,3]{1,0:T(4,128)S(1)} %convolution_bitcast_fusion), channel_id=1, replica_groups=mesh['cable'=4,'fx'=32,'fz'=2] {'cable','fx','fz'}, use_global_device_ids=true, to_apply=%region_22.23 | all-reduce | flops 9 | bytes 72 | tf_op jit(solution)/shard_map/psum | solution.py:128
  (194 shorter events, 46.8 us)
Async XLA Ops:
  10.5 26.7 %all-to-all-start = ((f32[64,1,1088]{2,1,0:T(1,128)}), f32[64,1,1088]{2,1,0:T(1,128)S(1)}, u32[]{:S(2)}, u32[]{:S(2)}) async-start(f32[64,1,1088]{2,1,0:T(1,128)} %reshape.922), calls=%async_computation | async-start | bytes 589824 | tf_op jit(solution)/shard_map/all_to_all | solution.py:88
  23.5 390.9 %reduce-scatter.10.cloned.1.call-start = ((), (), s32[]{:S(2)}) async-start(), calls=%async_computation.6 | async-start | bytes 2129920
  167.6 5.3 copy-start
  167.6 28.6 %copy-start.2 = (f32[8,16,128]{2,1,0:T(8,128)S(1)}, f32[8,16,128]{2,1,0:T(8,128)}, u32[]{:S(2)}) copy-start(f32[8,16,128]{2,1,0:T(8,128)} %param.9) | copy-start | bytes 196612
  172.9 4.1 collective-permute-start
  175.7 4.7 collective-permute-start.1
  180.4 3.4 collective-permute-start.3
  182.5 4.7 collective-permute-start.2
  187.4 6.5 collective-permute-start.4
  192.6 3.6 collective-permute-start.5
  201.1 77.7 %copy-start.5 = (f32[64]{0:T(128)S(1)}, f32[64]{0:T(128)}, u32[]{:S(2)}) copy-start(f32[64]{0:T(128)} %param.12) | copy-start | bytes 772
  201.1 214.2 %copy-start.3 = (f32[3,64]{1,0:T(4,128)S(1)}, f32[3,64]{1,0:T(4,128)}, u32[]{:S(2)}) copy-start(f32[3,64]{1,0:T(4,128)} %param.11) | copy-start | bytes 2308
  201.1 214.2 %copy-start.4 = (f32[3,64]{1,0:T(4,128)S(1)}, f32[3,64]{1,0:T(4,128)}, u32[]{:S(2)}) copy-start(f32[3,64]{1,0:T(4,128)} %param.10) | copy-start | bytes 2308
  278.3 539.9 %reduce-scatter.12.cloned.1.call-start = ((), (), s32[]{:S(2)}) async-start(), calls=%async_computation.7 | async-start | bytes 2129920
  576.5 4.8 collective-permute-start.6
  579.9 4.4 collective-permute-start.7
  584.4 3.9 collective-permute-start.9
  587.0 4.7 collective-permute-start.8
  591.9 6.6 collective-permute-start.10
  597.2 3.6 collective-permute-start.11
  682.9 614.4 %reduce-scatter.14.cloned.1.call-start = ((), (), s32[]{:S(2)}) async-start(), calls=%async_computation.8 | async-start | bytes 2129920
  1057.7 3.7 collective-permute-start.12
  1060.1 4.4 collective-permute-start.13
  1064.6 3.6 collective-permute-start.15
  1066.9 4.7 collective-permute-start.14
  1071.8 6.7 collective-permute-start.16
  1077.0 3.6 collective-permute-start.17
  1080.9 67.7 %copy-start.1 = (f32[3,8,16,128]{3,2,1,0:T(8,128)}, f32[3,8,16,128]{3,2,1,0:T(8,128)S(1)}, u32[]{:S(2)}) copy-start(f32[3,8,16,128]{3,2,1,0:T(8,128)S(1)} %fusion.13) | copy-start | bytes 589828
Sparse Core Ops, SparseCore 0:
  278.5 135.9 reduce-scatter.9
  683.0 135.1 reduce-scatter.11
  1162.8 134.4 reduce-scatter.13
